TPU v7x, 32 devices: a whole 2x2x4 slice. The times are simulated.
32 devices in a mesh: groups: 2 (over y), seq: 4 (over z), dp: 4 (over x, core).
Axes of the slice: x: 2, y: 2, z: 4, core: 2. Of those that a mesh axis runs over, the one named last changes fastest.
Arguments:
- inputs: bfloat16 [8, 4096, 448], P(('groups', 'dp'), 'seq'), parts along dimension 0, may hold values from -6 to 6
- cotangent: bfloat16 [8, 4096, 448], P(('groups', 'dp'), 'seq'), parts along dimension 0, may hold values from -6 to 6
- first_weight_matrix: bfloat16 [3, 448, 448], P(None, None, 'dp'), may hold values from -0.15625 to 0.15625
- weight_two: bfloat16 [3, 448, 448], P(None, None, 'dp'), may hold values from -0.15625 to 0.15625
Outputs:
- input_grad: bfloat16 [8, 4096, 448], P(('groups', 'dp'), 'seq'), parts along dimension 0
- grad_one: float32 [6, 448, 448], P('groups', None, 'dp'), parts along dimension 0
- grad_two: float32 [6, 448, 448], P('groups', None, 'dp'), parts along dimension 0
There are 2 independent parts, one for each index of `groups`. A program takes and returns all parts, laid end to end along the dimension named above; an argument that names none is the same for every part. Nothing has to cross between parts.
All inputs are finite; a program needn't handle non-finite values.
Results may differ from a plain program's by a relative error of at most 0.012.
Values may be sent and summed in bfloat16 or wider, within the bound.
No kernel may reach another device: no remote copies, remote signals or barrier semaphores. Data moves between devices by JAX's collectives and lax.ppermute only.
A program may use at most 64 MiB of HBM per device.

v0:
```python
import math
import jax
import jax.numpy as jnp
from jax import lax
from jax.sharding import PartitionSpec as P


def shifted(block, axis, distance):
    devices = range(lax.axis_size(axis))
    route = [(i - distance, i) for i in devices if i - distance in devices]
    return lax.ppermute(block, axis, route)


def gelu_slope(value):
    return jax.vjp(jax.nn.gelu, value)[1](jnp.ones_like(value))[0]


def outer_terms(left, right, factor):
    product = lax.dot_general(
        left, right, (((0,), (0,)), ((), ())), preferred_element_type=jnp.float32
    )
    return product * factor


def back_product(tap, weight):
    return lax.dot_general(
        tap, weight, (((1,), (1,)), ((), ())), preferred_element_type=jnp.float32
    )


def on_device(inputs, cotangent, first_weight_matrix, weight_two):
    chans = inputs.shape[2]
    rows = inputs.shape[0] * inputs.shape[1]
    factor = 1.0 / math.sqrt(
        inputs.shape[0] * lax.axis_size("dp") * inputs.shape[1] * lax.axis_size("seq")
    )
    full_one = lax.all_gather(first_weight_matrix, "dp", axis=2, tiled=True)
    flat_in = inputs.reshape(rows, chans)
    inputs_f = flat_in.astype(jnp.float32)
    input_activation = jax.nn.gelu(inputs_f).astype(jnp.bfloat16)
    act_before = shifted(input_activation, "seq", 2)
    act_after = shifted(input_activation, "seq", -2)
    flat_cot = cotangent.reshape(rows, chans)
    cot_later = shifted(flat_cot, "seq", -4)
    cot_earlier = shifted(flat_cot, "seq", 4)
    preactivation = jnp.dot(act_before, full_one[0], preferred_element_type=jnp.float32)
    preactivation = preactivation + jnp.dot(
        input_activation, full_one[1], preferred_element_type=jnp.float32
    )
    preactivation = preactivation + jnp.dot(
        act_after, full_one[2], preferred_element_type=jnp.float32
    )
    hidden_f = (inputs_f + preactivation).astype(jnp.bfloat16).astype(jnp.float32)
    act_one = jax.nn.gelu(hidden_f).astype(jnp.bfloat16)
    full_two = lax.all_gather(weight_two, "dp", axis=2, tiled=True)
    second_layer_taps = (cot_later, flat_cot, cot_earlier)
    delta_one = back_product(second_layer_taps[0], full_two[0])
    delta_one = delta_one + back_product(second_layer_taps[1], full_two[1])
    delta_one = delta_one + back_product(second_layer_taps[2], full_two[2])
    middle_gradient = (flat_cot.astype(jnp.float32) + gelu_slope(hidden_f) * delta_one).astype(
        jnp.bfloat16
    )
    part_two = jnp.stack(
        [outer_terms(act_one, second_layer_taps[k], factor) for k in range(3)]
    ).astype(jnp.bfloat16)
    grad_two = lax.psum(
        lax.psum_scatter(part_two, "dp", scatter_dimension=2, tiled=True).astype(jnp.float32), "seq"
    )
    grad_later = shifted(middle_gradient, "seq", -2)
    grad_earlier = shifted(middle_gradient, "seq", 2)
    first_layer_taps = (grad_later, middle_gradient, grad_earlier)
    delta_zero = back_product(first_layer_taps[0], full_one[0])
    delta_zero = delta_zero + back_product(first_layer_taps[1], full_one[1])
    delta_zero = delta_zero + back_product(first_layer_taps[2], full_one[2])
    input_grad = (middle_gradient.astype(jnp.float32) + gelu_slope(inputs_f) * delta_zero).astype(
        jnp.bfloat16
    )
    part_one = jnp.stack(
        [outer_terms(input_activation, first_layer_taps[k], factor) for k in range(3)]
    ).astype(jnp.bfloat16)
    grad_one = lax.psum(
        lax.psum_scatter(part_one, "dp", scatter_dimension=2, tiled=True).astype(jnp.float32), "seq"
    )
    return (input_grad.reshape(inputs.shape), grad_one, grad_two)


def solution(mesh):
    placed = (
        P(("groups", "dp"), "seq", None),
        P(("groups", "dp"), "seq", None),
        P(None, None, "dp"),
        P(None, None, "dp"),
    )
    return jax.shard_map(
        on_device,
        mesh=mesh,
        in_specs=placed,
        out_specs=(
            P(("groups", "dp"), "seq", None),
            P("groups", None, "dp"),
            P("groups", None, "dp"),
        ),
        check_vma=False,
    )
```

profile of v0, /device:TPU:0, one launch (start us, length us, event | category | flops | bytes accessed | tf_op | source)
XLA Modules:
  0.0 242.5 jit_solution(234301999639612765)
XLA Ops:
  7.2 2.2 copy.9
  9.5 2.1 copy.13
  11.7 1.6 fusion.26
  13.2 6.9 %collective-permute-start = (bf16[1024,448]{0,1:T(8,128)(2,1)}, bf16[1024,448]{0,1:T(8,128)(2,1)}, u32[]{:S(2)}, u32[]{:S(2)}) collective-permute-start(bf16[1024,448]{0,1:T(8,128)(2,1)} %fusion.26), channel_id=1, source_target_pairs={{0,8},{4,12},{1,9},{5,13},{2,10},{6,14},{3,11},{7,15},{16,24},{20,... | collective-permute-start | bytes 2752520 | tf_op jit(solution)/shard_map/ppermute | solution.py:11
  20.1 1.3 collective-permute-start.1
  21.4 1.6 collective-permute-start.2
  23.0 11.0 %all-gather.3.cloned.1.call-done = bf16[3,448,448]{1,0,2:T(4,128)(2,1)} async-done(((bf16[3,448,112]{1,0,2:T(4,128)(2,1)}), bf16[3,448,448]{1,0,2:T(4,128)(2,1)}) %all-gather.3.cloned.1.call-update) | async-done | bytes 1204240 | tf_op jit(solution)/shard_map/all_gather | solution.py:37
  34.0 6.1 %fusion.88 = (bf16[1,448,448]{1,0,2:T(2,128)(2,1)S(1)}, bf16[1,448,448]{1,0,2:T(2,128)(2,1)S(1)}, bf16[1,448,448]{1,0,2:T(2,128)(2,1)}) fusion(bf16[3,448,448]{1,0,2:T(4,128)(2,1)} %all-gather.3.cloned.1.call-done), kind=kLoop, calls=%fused_computation.93 | loop fusion | bytes 2408448 | tf_op jit(solution)/shard_map/slice | solution.py:51
  40.1 17.2 %all-gather.5.cloned.1.call-done = bf16[3,448,448]{1,0,2:T(4,128)(2,1)} async-done(((bf16[3,448,112]{1,0,2:T(4,128)(2,1)}), bf16[3,448,448]{1,0,2:T(4,128)(2,1)}) %all-gather.5.cloned.1.call-update) | async-done | bytes 1204240 | tf_op jit(solution)/shard_map/all_gather | solution.py:55
  57.3 6.3 %fusion.87 = (bf16[1,448,448]{1,0,2:T(2,128)(2,1)}, bf16[1,448,448]{1,0,2:T(2,128)(2,1)}, bf16[1,448,448]{1,0,2:T(2,128)(2,1)}) fusion(bf16[3,448,448]{1,0,2:T(4,128)(2,1)} %all-gather.5.cloned.1.call-done), kind=kLoop, calls=%fused_computation.92 | loop fusion | bytes 2408448 | tf_op jit(solution)/shard_map/slice | solution.py:59
  63.6 2.4 copy.21
  66.0 2.0 copy.22
  68.0 1.9 copy.23
  69.9 3.5 %copy.24 = bf16[1,448,448]{2,1,0:T(8,128)(2,1)} copy(bf16[1,448,448]{1,0,2:T(2,128)(2,1)} %get-tuple-element.7) | data formatting | bytes 802816
  73.4 1.3 copy.25
  74.7 1.0 fusion.46
  75.7 3.1 %fusion.57 = f32[1024,448]{0,1:T(8,128)} fusion(bf16[1,448,448]{2,1,0:T(8,128)(2,1)S(1)} %copy.25, bf16[1,1024,448]{1,2,0:T(8,128)(2,1)} %param.5), kind=kOutput, calls=%fused_computation.71 | convolution fusion | flops 411041792 | bytes 3153920 | tf_op jit(solution)/shard_map/dot_general | solution.py:26
  78.8 1.9 fusion.74
  80.8 2.1 fusion.27
  82.8 2.3 fusion.40
  85.2 2.0 fusion.41
  87.4 1.8 copy.19
  89.2 2.5 %reshape.22 = bf16[448,1344]{1,0:T(8,128)(2,1)} reshape(bf16[448,3,448]{2,1,0:T(4,128)(2,1)S(1)} %bitcast.119) | data formatting | bytes 2408448
  92.0 3.2 %fusion.59 = f32[1024,448]{0,1:T(8,128)} fusion(bf16[1024,448]{0,1:T(8,128)(2,1)} %collective-permute-done.2, bf16[1,448,448]{2,1,0:T(8,128)(2,1)S(1)} %copy-done.10), kind=kOutput, calls=%fused_computation.73 | convolution fusion | flops 411041792 | bytes 3153920 | tf_op jit(solution)/shard_map/dot_general | solution.py:26
  95.2 1.3 copy.26
  96.5 4.2 %fusion.17 = bf16[1024,448]{0,1:T(8,128)(2,1)S(1)} fusion(bf16[1024,448]{0,1:T(8,128)(2,1)} %copy-done.17, f32[1024,448]{0,1:T(8,128)} %fusion.59, f32[1024,448]{0,1:T(8,128)S(1)} %copy-done.7, bf16[1024,448]{0,1:T(8,128)(2,1)} %collective-permute-done.2, bf16[1,448,448]{2,1,0:T(8,128)(2,1)S(1)} %copy.26, bf16[1,1024,448]{1,2,0:T(8,128)(2,1)} %param.5), kind=kOutput, calls=%fused_computation.27 | convolution fusion | flops 422051840 | bytes 7741440 | tf_op jit(solution)/shard_map/dot_general | solution.py:26
  100.7 4.5 %collective-permute-start.4 = (bf16[1024,448]{0,1:T(8,128)(2,1)S(1)}, bf16[1024,448]{0,1:T(8,128)(2,1)S(1)}, u32[]{:S(2)}, u32[]{:S(2)}) collective-permute-start(bf16[1024,448]{0,1:T(8,128)(2,1)S(1)} %fusion.17), channel_id=1, source_target_pairs={{0,8},{4,12},{1,9},{5,13},{2,10},{6,14},{3,11},{7,15},{16,24},{20,... | collective-permute-start | bytes 2752520 | tf_op jit(solution)/shard_map/ppermute | solution.py:11
  105.2 1.3 collective-permute-start.3
  106.5 0.8 fusion.43
  107.4 17.8 %collective-permute-done.4 = bf16[1024,448]{0,1:T(8,128)(2,1)S(1)} collective-permute-done((bf16[1024,448]{0,1:T(8,128)(2,1)S(1)}, bf16[1024,448]{0,1:T(8,128)(2,1)S(1)}, u32[]{:S(2)}, u32[]{:S(2)}) %collective-permute-start.4) | collective-permute-done | bytes 917536 | tf_op jit(solution)/shard_map/ppermute | solution.py:11
  125.2 0.8 fusion.42
  126.1 23.8 %collective-permute-done.3 = bf16[1024,448]{0,1:T(8,128)(2,1)S(1)} collective-permute-done((bf16[1024,448]{0,1:T(8,128)(2,1)S(1)}, bf16[1024,448]{0,1:T(8,128)(2,1)S(1)}, u32[]{:S(2)}, u32[]{:S(2)}) %collective-permute-start.3) | collective-permute-done | bytes 917536 | tf_op jit(solution)/shard_map/ppermute | solution.py:11
  149.9 0.9 copy-done.15
  150.8 0.8 fusion.44
  151.8 1.8 copy.17
  153.6 2.5 %reshape.20 = bf16[448,1344]{1,0:T(8,128)(2,1)} reshape(bf16[448,3,448]{2,1,0:T(4,128)(2,1)S(1)} %bitcast.120) | data formatting | bytes 2408448
  156.2 0.6 fusion.69
  156.9 0.4 copy-done.1
  157.5 0.6 fusion.72
  158.2 0.5 copy-done.4
  158.8 0.5 copy-done.19
  159.3 2.7 %fusion.52 = bf16[1,1024,448]{1,2,0:T(8,128)(2,1)} fusion(f32[1024,448]{0,1:T(8,128)S(1)} %fusion.72, f32[1024,448]{0,1:T(8,128)S(1)} %fusion.69, bf16[1,1024,448]{1,2,0:T(8,128)(2,1)S(1)} %copy-done.4, bf16[1024,448]{0,1:T(8,128)(2,1)S(1)} %copy-done.14, bf16[1024,448]{0,1:T(8,128)(2,1)S(1)} %copy-done.19, bf16[1,448,448]{2,1,0:T(8,128)(2,1)S(1)} %copy-done.12), kind=kOutput, calls=%fused_computation.68 | convolution fusion | flops 422051840 | bytes 7741440 | tf_op jit(solution)/shard_map/dot_general | solution.py:26
  162.0 1.7 reshape.23
  163.7 0.3 copy.20
  164.0 15.7 %reduce-scatter.7.cloned.1.call-done = bf16[112,1344]{1,0:T(8,128)(2,1)} async-done(((bf16[448,1344]{1,0:T(8,128)(2,1)}), bf16[112,1344]{1,0:T(8,128)(2,1)}) %reduce-scatter.7.cloned.1.call-update) | async-done | bytes 301072
  179.8 1.7 reshape.21
  181.5 0.3 copy.18
  181.8 54.2 %all-reduce.2 = (f32[3,448,112]{2,1,0:T(8,128)}, f32[3,448,112]{2,1,0:T(8,128)}) all-reduce(bf16[3,448,112]{2,1,0:T(8,128)(2,1)S(1)} %copy.18, bf16[3,448,112]{2,1,0:T(8,128)(2,1)S(1)} %copy.20), channel_id=1, replica_groups=mesh['groups'=2,'seq'=4,'dp'=4] {'seq'}, use_global_device_ids=true, to_apply=%region_1.0 | all-reduce | flops 301056 | bytes 1806336 | tf_op jit(solution)/shard_map/psum | solution.py:81
  (50 shorter events, 1.4 us)
Async XLA Ops:
  7.2 4.5 %copy-start.2 = (bf16[1,1024,448]{1,2,0:T(8,128)(2,1)S(1)}, bf16[1,1024,448]{1,2,0:T(8,128)(2,1)}, u32[]{:S(2)}) copy-start(bf16[1,1024,448]{1,2,0:T(8,128)(2,1)} %param.4) | copy-start | bytes 2752516
  7.2 26.8 %all-gather.3.cloned.1.call-start = ((), (), s32[]{:S(2)}) async-start(), calls=%async_computation.2 | async-start | bytes 2293760 | tf_op jit(solution)/shard_map/all_gather | solution.py:37
  9.4 47.9 %all-gather.5.cloned.1.call-start = ((), (), s32[]{:S(2)}) async-start(), calls=%async_computation.3 | async-start | bytes 2293760 | tf_op jit(solution)/shard_map/all_gather | solution.py:55
  11.6 150.4 %reduce-scatter.9.cloned.1.call-start = ((), (), s32[]{:S(2)}) async-start(), calls=%async_computation.5 | async-start | bytes 1576960
  13.2 65.6 %collective-permute-start = (bf16[1024,448]{0,1:T(8,128)(2,1)}, bf16[1024,448]{0,1:T(8,128)(2,1)}, u32[]{:S(2)}, u32[]{:S(2)}) collective-permute-start(bf16[1024,448]{0,1:T(8,128)(2,1)} %fusion.26), channel_id=1, source_target_pairs={{0,8},{4,12},{1,9},{5,13},{2,10},{6,14},{3,11},{7,15},{16,24},{20,... | collective-permute-start | bytes 2752520 | tf_op jit(solution)/shard_map/ppermute | solution.py:11
  20.1 60.7 %collective-permute-start.1 = (bf16[1024,448]{0,1:T(8,128)(2,1)}, bf16[1024,448]{0,1:T(8,128)(2,1)}, u32[]{:S(2)}, u32[]{:S(2)}) collective-permute-start(bf16[1024,448]{0,1:T(8,128)(2,1)} %fusion.26), channel_id=1, source_target_pairs={{8,0},{12,4},{9,1},{13,5},{10,2},{14,6},{11,3},{15,7},{24,16},{28,... | collective-permute-start | bytes 2752520 | tf_op jit(solution)/shard_map/ppermute | solution.py:11
  21.4 63.8 %collective-permute-start.2 = (bf16[1024,448]{0,1:T(8,128)(2,1)}, bf16[1024,448]{0,1:T(8,128)(2,1)}, u32[]{:S(2)}, u32[]{:S(2)}) collective-permute-start(bf16[1024,448]{0,1:T(8,128)(2,1)} %bitcast), channel_id=1, source_target_pairs={} | collective-permute-start | bytes 2752520 | tf_op jit(solution)/shard_map/ppermute | solution.py:11
  66.0 12.8 %copy-start = (bf16[1,448,448]{2,1,0:T(8,128)(2,1)}, bf16[1,448,448]{2,1,0:T(8,128)(2,1)S(1)}, u32[]{:S(2)}) copy-start(bf16[1,448,448]{2,1,0:T(8,128)(2,1)S(1)} %copy.21) | copy-start | bytes 1204228
  68.0 5.4 %copy-start.6 = (bf16[1,448,448]{1,0,2:T(2,128)(2,1)S(1)}, bf16[1,448,448]{1,0,2:T(2,128)(2,1)}, u32[]{:S(2)}) copy-start(bf16[1,448,448]{1,0,2:T(2,128)(2,1)} %get-tuple-element.6) | copy-start | bytes 1204228
  69.9 4.8 %copy-start.8 = (bf16[1,448,448]{2,1,0:T(8,128)(2,1)S(1)}, bf16[1,448,448]{2,1,0:T(8,128)(2,1)}, u32[]{:S(2)}) copy-start(bf16[1,448,448]{2,1,0:T(8,128)(2,1)} %copy.22) | copy-start | bytes 1204228
  78.8 1.9 copy-start.11
  82.8 2.4 copy-start.17
  89.2 2.8 %copy-start.10 = (bf16[1,448,448]{2,1,0:T(8,128)(2,1)S(1)}, bf16[1,448,448]{2,1,0:T(8,128)(2,1)}, u32[]{:S(2)}) copy-start(bf16[1,448,448]{2,1,0:T(8,128)(2,1)} %copy.24) | copy-start | bytes 1204228
  91.7 3.4 %copy-start.5 = (bf16[1,448,448]{1,0,2:T(2,128)(2,1)S(1)}, bf16[1,448,448]{1,0,2:T(2,128)(2,1)}, u32[]{:S(2)}) copy-start(bf16[1,448,448]{1,0,2:T(2,128)(2,1)} %get-tuple-element.5) | copy-start | bytes 1204228
  91.7 4.8 %copy-start.7 = (f32[1024,448]{0,1:T(8,128)S(1)}, f32[1024,448]{0,1:T(8,128)}, u32[]{:S(2)}) copy-start(f32[1024,448]{0,1:T(8,128)} %fusion.57) | copy-start | bytes 5505028
  91.8 88.0 %reduce-scatter.7.cloned.1.call-start = ((), (), s32[]{:S(2)}) async-start(), calls=%async_computation.4 | async-start | bytes 1576960
  96.5 10.0 %copy-start.3 = (bf16[1,1024,448]{1,2,0:T(8,128)(2,1)S(1)}, bf16[1,1024,448]{1,2,0:T(8,128)(2,1)}, u32[]{:S(2)}) copy-start(bf16[1,1024,448]{1,2,0:T(8,128)(2,1)} %param.4) | copy-start | bytes 2752516
  100.7 6.7 %copy-start.13 = (bf16[1024,448]{0,1:T(8,128)(2,1)}, bf16[1024,448]{0,1:T(8,128)(2,1)S(1)}, u32[]{:S(2)}) copy-start(bf16[1024,448]{0,1:T(8,128)(2,1)S(1)} %fusion.17) | copy-start | bytes 2752516
  100.7 24.5 %collective-permute-start.4 = (bf16[1024,448]{0,1:T(8,128)(2,1)S(1)}, bf16[1024,448]{0,1:T(8,128)(2,1)S(1)}, u32[]{:S(2)}, u32[]{:S(2)}) collective-permute-start(bf16[1024,448]{0,1:T(8,128)(2,1)S(1)} %fusion.17), channel_id=1, source_target_pairs={{0,8},{4,12},{1,9},{5,13},{2,10},{6,14},{3,11},{7,15},{16,24},{20,... | collective-permute-start | bytes 2752520 | tf_op jit(solution)/shard_map/ppermute | solution.py:11
  105.2 44.7 %collective-permute-start.3 = (bf16[1024,448]{0,1:T(8,128)(2,1)S(1)}, bf16[1024,448]{0,1:T(8,128)(2,1)S(1)}, u32[]{:S(2)}, u32[]{:S(2)}) collective-permute-start(bf16[1024,448]{0,1:T(8,128)(2,1)S(1)} %fusion.17), channel_id=1, source_target_pairs={{8,0},{12,4},{9,1},{13,5},{10,2},{14,6},{11,3},{15,7},{24,16},{28,... | collective-permute-start | bytes 2752520 | tf_op jit(solution)/shard_map/ppermute | solution.py:11
  125.2 0.9 copy-start.18
  149.9 0.9 copy-start.15
  153.6 2.5 %copy-start.9 = (bf16[1,448,448]{2,1,0:T(8,128)(2,1)S(1)}, bf16[1,448,448]{2,1,0:T(8,128)(2,1)}, u32[]{:S(2)}) copy-start(bf16[1,448,448]{2,1,0:T(8,128)(2,1)} %copy.22) | copy-start | bytes 1204228
  153.6 2.5 %copy-start.14 = (bf16[1024,448]{0,1:T(8,128)(2,1)S(1)}, bf16[1024,448]{0,1:T(8,128)(2,1)}, u32[]{:S(2)}) copy-start(bf16[1024,448]{0,1:T(8,128)(2,1)} %copy-done.13) | copy-start | bytes 2752516
  156.2 1.0 copy-start.1
  156.2 1.3 copy-start.16
  157.5 1.2 copy-start.4
  157.5 1.3 copy-start.12
  157.5 1.8 copy-start.19
Sparse Core Ops, SparseCore 0:
  10.1 23.8 all-gather.2
  36.1 21.1 all-gather.4
  91.9 26.2 reduce-scatter.8
  156.3 23.4 reduce-scatter.6
where the time goes:
time: 243 us
  waiting for transfers between devices  85.6 us (35%)
  blocking collectives  54.2 us (22%)
  local copies, waits for them, and re-layouts  44.6 us (18%)
  matrix products  26.1 us (11%)
  starting transfers between devices  15.9 us (7%)
  between operations  14.1 us (6%)
    psum x1, blocking collectives, on_device(): lax.psum(lax.psum_scatter(part_one, 'dp', scatter_dimension=2, tiled=True...  54.2 us
    ppermute x5, waiting for transfers between devices, shifted(): return lax.ppermute(block, axis, route)  41.6 us
    unnamed x56, local copies, waits for them, and re-layouts  32.2 us
    all_gather x1, waiting for transfers between devices, on_device(): full_two = lax.all_gather(weight_two, 'dp', axis=2, tiled=True)  17.2 us
    unnamed x6, waiting for transfers between devices  15.8 us
    ppermute x5, starting transfers between devices, shifted(): return lax.ppermute(block, axis, route)  15.6 us
    dot_general x6, matrix products, back_product(): lax.dot_general(tap, weight, (((1,), (1,)), ((), ())), preferred_element_...  14.4 us
    all_gather x1, waiting for transfers between devices, on_device(): full_one = lax.all_gather(first_weight_matrix, 'dp', axis=2, tiled=True)  11 us
  transfers between devices with their start and end apart: 9, of which 5 were waited for; matrix products, arithmetic and copies ran while one was open for 24% of the time, Pallas kernels for 0%

commit v1 on v0

--- a/solution.py
+++ b/solution.py
@@ -3,6 +3,18 @@
 import jax.numpy as jnp
 from jax import lax
 from jax.sharding import PartitionSpec as P
+
+
+def gather_by_bits(x, axis, dim):
+    ways, here = (lax.axis_size(axis), lax.axis_index(axis))
+    grown, reach = (x, 1)
+    while reach < ways:
+        theirs = lax.ppermute(grown, axis, [(d, d ^ reach) for d in range(ways)])
+        mine_first = jnp.concatenate([grown, theirs], axis=dim)
+        theirs_first = jnp.concatenate([theirs, grown], axis=dim)
+        grown = jnp.where(here & reach == 0, mine_first, theirs_first)
+        reach = 2 * reach
+    return grown
 
 
 def shifted(block, axis, distance):
@@ -52,7 +64,7 @@
     )
     hidden_f = (inputs_f + preactivation).astype(jnp.bfloat16).astype(jnp.float32)
     act_one = jax.nn.gelu(hidden_f).astype(jnp.bfloat16)
-    full_two = lax.all_gather(weight_two, "dp", axis=2, tiled=True)
+    full_two = gather_by_bits(weight_two, "dp", 2)
     second_layer_taps = (cot_later, flat_cot, cot_earlier)
     delta_one = back_product(second_layer_taps[0], full_two[0])
     delta_one = delta_one + back_product(second_layer_taps[1], full_two[1])

time: 243 us -> 222 us (0.914)
  local copies, waits for them, and re-layouts: 44.6 us -> 29.7 us
  waiting for transfers between devices: 85.6 us -> 78.4 us
  other arithmetic: 1.96 us -> 4.7 us
    all_gather x1 -> x0, waiting for transfers between devices: 17.2 us -> none  [on_device(): full_two = lax.all_gather(weight_two, 'dp', axis=2, tiled=True)]
    ppermute x0 -> x2, waiting for transfers between devices: none -> 16.8 us  [gather_by_bits(): theirs = lax.ppermute(grown, axis, [(d, d ^ reach) for d in range(ways)])]
    all_gather x1, waiting for transfers between devices: 11 us -> 0.01 us  [on_device(): full_one = lax.all_gather(first_weight_matrix, 'dp', axis=2, tiled=True)]
    unnamed x56 -> x50, local copies, waits for them, and re-layouts: 32.2 us -> 23.6 us
    slice x1 -> x0, local copies, waits for them, and re-layouts: 6.33 us -> none  [on_device(): delta_one = delta_one + back_product(second_layer_taps[2], full_two[2])]
    ppermute x5, starting transfers between devices: 15.6 us -> 11.1 us  [shifted(): return lax.ppermute(block, axis, route)]
    ppermute x5, waiting for transfers between devices: 41.6 us -> 45.7 us  [shifted(): return lax.ppermute(block, axis, route)]
    ppermute x0 -> x2, starting transfers between devices: none -> 3.44 us  [gather_by_bits(): theirs = lax.ppermute(grown, axis, [(d, d ^ reach) for d in range(ways)])]
  transfers between devices with their start and end apart: 9 -> 10, of which waited for: 5 -> 6; matrix products, arithmetic and copies ran while one was open for 24% -> 21% of each run, Pallas kernels for 0% -> 0%
where the time goes in v1:
time: 222 us; the launch traced here: 221 us
  waiting for transfers between devices  78.4 us (35%)
  blocking collectives  54.2 us (24%)
  local copies, waits for them, and re-layouts  29.7 us (13%)
  matrix products  25.2 us (11%)
  starting transfers between devices  14.9 us (7%)
  between operations  14.1 us (6%)
  other arithmetic  4.7 us (2%)
    psum x1, blocking collectives, on_device(): lax.psum(lax.psum_scatter(part_one, 'dp', scatter_dimension=2, tiled=True...  54.2 us
    ppermute x5, waiting for transfers between devices, shifted(): return lax.ppermute(block, axis, route)  45.7 us
    unnamed x50, local copies, waits for them, and re-layouts  23.6 us
    ppermute x2, waiting for transfers between devices, gather_by_bits(): theirs = lax.ppermute(grown, axis, [(d, d ^ reach) for d in range(ways)])  16.8 us
    unnamed x5, waiting for transfers between devices  15.9 us
    dot_general x6, matrix products, back_product(): lax.dot_general(tap, weight, (((1,), (1,)), ((), ())), preferred_element_...  12.3 us
    ppermute x5, starting transfers between devices, shifted(): return lax.ppermute(block, axis, route)  11.1 us
    dot_general x5, matrix products, outer_terms(): lax.dot_general(left, right, (((0,), (0,)), ((), ())), preferred_element_...  6.8 us
  transfers between devices with their start and end apart: 10, of which 6 were waited for; matrix products, arithmetic and copies ran while one was open for 21% of the time, Pallas kernels for 0%

profile of v1, /device:TPU:0, one launch (start us, length us, event | category | flops | bytes accessed | tf_op | source)
XLA Modules:
  0.0 221.1 jit_solution(16981940895626397216)
XLA Ops:
  7.2 2.2 copy.8
  9.5 0.5 collective-permute-start.2
  10.0 1.5 collective-permute-done.2
  11.5 1.7 maximum_select_fusion.1
  13.2 2.9 %collective-permute-start.3 = (bf16[3,448,224]{2,1,0:T(8,128)(2,1)S(1)}, bf16[3,448,224]{2,1,0:T(8,128)(2,1)S(1)}, u32[]{:S(2)}, u32[]{:S(2)}) collective-permute-start(bf16[3,448,224]{2,1,0:T(8,128)(2,1)S(1)} %maximum_select_fusion.1), channel_id=1, source_target_pairs={{0,2},{1,3},{2,0},{3,1},{4,6},{5,7},{6,4},{7,5},{8,10},{9,11},{10,... | collective-permute-start | bytes 1806344 | tf_op jit(solution)/shard_map/ppermute | solution.py:12
  16.1 1.6 fusion.26
  17.6 5.4 %collective-permute-start = (bf16[1024,448]{0,1:T(8,128)(2,1)}, bf16[1024,448]{0,1:T(8,128)(2,1)}, u32[]{:S(2)}, u32[]{:S(2)}) collective-permute-start(bf16[1024,448]{0,1:T(8,128)(2,1)} %fusion.26), channel_id=1, source_target_pairs={{0,8},{4,12},{1,9},{5,13},{2,10},{6,14},{3,11},{7,15},{16,24},{20,... | collective-permute-start | bytes 2752520 | tf_op jit(solution)/shard_map/ppermute | solution.py:23
  23.1 1.3 collective-permute-start.1
  24.4 1.6 collective-permute-start.4
  26.0 15.3 %collective-permute-done.3 = bf16[3,448,224]{2,1,0:T(8,128)(2,1)S(1)} collective-permute-done((bf16[3,448,224]{2,1,0:T(8,128)(2,1)S(1)}, bf16[3,448,224]{2,1,0:T(8,128)(2,1)S(1)}, u32[]{:S(2)}, u32[]{:S(2)}) %collective-permute-start.3) | collective-permute-done | bytes 602144 | tf_op jit(solution)/shard_map/ppermute | solution.py:12
  41.3 1.1 maximum_select_fusion
  42.4 1.1 copy-done.2
  43.5 3.1 %fusion.54 = f32[448,1024]{1,0:T(8,128)} fusion(bf16[3,448,448]{2,1,0:T(8,128)(2,1)S(1)} %maximum_select_fusion, bf16[1,1024,448]{1,2,0:T(8,128)(2,1)} %param.5), kind=kOutput, calls=%fused_computation.74 | convolution fusion | flops 411041792 | bytes 3211264 | tf_op jit(solution)/shard_map/dot_general | solution.py:38
  46.6 6.1 %fusion.82 = (bf16[1,448,448]{1,0,2:T(2,128)(2,1)S(1)}, bf16[1,448,448]{1,0,2:T(2,128)(2,1)S(1)}, bf16[1,448,448]{1,0,2:T(2,128)(2,1)}) fusion(bf16[3,448,448]{1,0,2:T(4,128)(2,1)} %all-gather.2.cloned.1.call-done), kind=kLoop, calls=%fused_computation.94 | loop fusion | bytes 2408448 | tf_op jit(solution)/shard_map/slice | solution.py:63
  52.6 2.4 %copy.16 = bf16[1,448,448]{2,1,0:T(8,128)(2,1)S(1)} copy(bf16[1,448,448]{1,0,2:T(2,128)(2,1)} %get-tuple-element.7) | data formatting | bytes 802816
  55.0 2.0 copy.17
  57.0 1.3 copy.18
  58.3 2.2 fusion.46
  60.5 1.9 fusion.69
  62.4 5.3 %collective-permute-done.1 = bf16[1024,448]{0,1:T(8,128)(2,1)} collective-permute-done((bf16[1024,448]{0,1:T(8,128)(2,1)}, bf16[1024,448]{0,1:T(8,128)(2,1)}, u32[]{:S(2)}, u32[]{:S(2)}) %collective-permute-start.1) | collective-permute-done | bytes 917536 | tf_op jit(solution)/shard_map/ppermute | solution.py:23
  67.7 2.1 fusion.27
  69.7 2.3 %fusion.40 = bf16[1,448,448]{2,1,0:T(8,128)(2,1)S(1)} fusion(bf16[1,1024,448]{1,2,0:T(8,128)(2,1)} %param.5, bf16[1024,448]{0,1:T(8,128)(2,1)S(1)} %fusion.27), kind=kOutput, calls=%fused_computation.58 | convolution fusion | flops 416030720 | bytes 2236416 | tf_op jit(solution)/shard_map/dot_general | solution.py:31
  72.1 2.0 fusion.41
  74.3 1.8 copy.14
  76.1 2.5 %reshape.22 = bf16[448,1344]{1,0:T(8,128)(2,1)} reshape(bf16[448,3,448]{2,1,0:T(4,128)(2,1)S(1)} %bitcast.121) | data formatting | bytes 2408448
  78.9 2.0 fusion.55
  80.9 3.3 %fusion.17 = bf16[1024,448]{0,1:T(8,128)(2,1)S(1)} fusion(bf16[1024,448]{0,1:T(8,128)(2,1)S(1)} %copy-done.16, f32[448,1024]{1,0:T(8,128)S(1)} %fusion.55, f32[448,1024]{1,0:T(8,128)S(1)} %copy-done.7, bf16[1024,448]{0,1:T(8,128)(2,1)} %collective-permute-done.4, bf16[3,448,448]{2,1,0:T(8,128)(2,1)S(1)} %copy-done.3, bf16[1,1024,448]{1,2,0:T(8,128)(2,1)} %param.5), kind=kOutput, calls=%fused_computation.27 | convolution fusion | flops 422051840 | bytes 7798784 | tf_op jit(solution)/shard_map/dot_general | solution.py:38
  84.2 1.5 collective-permute-start.6
  85.7 1.3 collective-permute-start.5
  87.0 0.8 fusion.43
  87.8 16.7 %collective-permute-done.6 = bf16[1024,448]{0,1:T(8,128)(2,1)S(1)} collective-permute-done((bf16[1024,448]{0,1:T(8,128)(2,1)S(1)}, bf16[1024,448]{0,1:T(8,128)(2,1)S(1)}, u32[]{:S(2)}, u32[]{:S(2)}) %collective-permute-start.6) | collective-permute-done | bytes 917536 | tf_op jit(solution)/shard_map/ppermute | solution.py:23
  104.5 0.8 fusion.42
  105.5 23.7 %collective-permute-done.5 = bf16[1024,448]{0,1:T(8,128)(2,1)S(1)} collective-permute-done((bf16[1024,448]{0,1:T(8,128)(2,1)S(1)}, bf16[1024,448]{0,1:T(8,128)(2,1)S(1)}, u32[]{:S(2)}, u32[]{:S(2)}) %collective-permute-start.5) | collective-permute-done | bytes 917536 | tf_op jit(solution)/shard_map/ppermute | solution.py:23
  129.2 0.8 fusion.44
  130.3 1.8 copy.12
  132.1 2.5 %reshape.20 = bf16[448,1344]{1,0:T(8,128)(2,1)} reshape(bf16[448,3,448]{2,1,0:T(4,128)(2,1)S(1)} %bitcast.122) | data formatting | bytes 2408448
  134.7 0.6 fusion.64
  135.3 0.4 copy-done.1
  136.0 0.6 fusion.67
  136.6 0.5 copy-done.6
  137.3 0.4 copy-done.18
  137.7 2.7 %fusion.52 = bf16[1,1024,448]{1,2,0:T(8,128)(2,1)} fusion(f32[1024,448]{0,1:T(8,128)S(1)} %fusion.67, f32[1024,448]{0,1:T(8,128)S(1)} %fusion.64, bf16[1,1024,448]{1,2,0:T(8,128)(2,1)S(1)} %copy-done.6, bf16[1024,448]{0,1:T(8,128)(2,1)S(1)} %copy-done.12, bf16[1024,448]{0,1:T(8,128)(2,1)S(1)} %copy-done.18, bf16[1,448,448]{2,1,0:T(8,128)(2,1)S(1)} %copy-done.10), kind=kOutput, calls=%fused_computation.69 | convolution fusion | flops 422051840 | bytes 7741440 | tf_op jit(solution)/shard_map/dot_general | solution.py:38
  140.4 1.7 reshape.23
  142.2 0.3 copy.15
  142.5 15.8 %reduce-scatter.7.cloned.1.call-done = bf16[112,1344]{1,0:T(8,128)(2,1)} async-done(((bf16[448,1344]{1,0:T(8,128)(2,1)}), bf16[112,1344]{1,0:T(8,128)(2,1)}) %reduce-scatter.7.cloned.1.call-update) | async-done | bytes 301072
  158.3 1.7 reshape.21
  160.0 0.3 copy.13
  160.4 54.2 %all-reduce.2 = (f32[3,448,112]{2,1,0:T(8,128)}, f32[3,448,112]{2,1,0:T(8,128)}) all-reduce(bf16[3,448,112]{2,1,0:T(8,128)(2,1)S(1)} %copy.13, bf16[3,448,112]{2,1,0:T(8,128)(2,1)S(1)} %copy.15), channel_id=1, replica_groups=mesh['groups'=2,'seq'=4,'dp'=4] {'seq'}, use_global_device_ids=true, to_apply=%region_1.2 | all-reduce | flops 301056 | bytes 1806336 | tf_op jit(solution)/shard_map/psum | solution.py:93
  (46 shorter events, 1.5 us)
Async XLA Ops:
  7.2 8.9 %copy-start.4 = (bf16[1,1024,448]{1,2,0:T(8,128)(2,1)S(1)}, bf16[1,1024,448]{1,2,0:T(8,128)(2,1)}, u32[]{:S(2)}) copy-start(bf16[1,1024,448]{1,2,0:T(8,128)(2,1)} %param.4) | copy-start | bytes 2752516
  7.2 39.4 %all-gather.2.cloned.1.call-start = ((), (), s32[]{:S(2)}) async-start(), calls=%async_computation.2 | async-start | bytes 2293760 | tf_op jit(solution)/shard_map/all_gather | solution.py:49
  9.4 131.0 %reduce-scatter.9.cloned.1.call-start = ((), (), s32[]{:S(2)}) async-start(), calls=%async_computation.4 | async-start | bytes 1576960
  9.5 2.0 collective-permute-start.2
  13.2 28.2 %collective-permute-start.3 = (bf16[3,448,224]{2,1,0:T(8,128)(2,1)S(1)}, bf16[3,448,224]{2,1,0:T(8,128)(2,1)S(1)}, u32[]{:S(2)}, u32[]{:S(2)}) collective-permute-start(bf16[3,448,224]{2,1,0:T(8,128)(2,1)S(1)} %maximum_select_fusion.1), channel_id=1, source_target_pairs={{0,2},{1,3},{2,0},{3,1},{4,6},{5,7},{6,4},{7,5},{8,10},{9,11},{10,... | collective-permute-start | bytes 1806344 | tf_op jit(solution)/shard_map/ppermute | solution.py:12
  17.6 42.9 %collective-permute-start = (bf16[1024,448]{0,1:T(8,128)(2,1)}, bf16[1024,448]{0,1:T(8,128)(2,1)}, u32[]{:S(2)}, u32[]{:S(2)}) collective-permute-start(bf16[1024,448]{0,1:T(8,128)(2,1)} %fusion.26), channel_id=1, source_target_pairs={{0,8},{4,12},{1,9},{5,13},{2,10},{6,14},{3,11},{7,15},{16,24},{20,... | collective-permute-start | bytes 2752520 | tf_op jit(solution)/shard_map/ppermute | solution.py:23
  23.1 44.6 %collective-permute-start.1 = (bf16[1024,448]{0,1:T(8,128)(2,1)}, bf16[1024,448]{0,1:T(8,128)(2,1)}, u32[]{:S(2)}, u32[]{:S(2)}) collective-permute-start(bf16[1024,448]{0,1:T(8,128)(2,1)} %fusion.26), channel_id=1, source_target_pairs={{8,0},{12,4},{9,1},{13,5},{10,2},{14,6},{11,3},{15,7},{24,16},{28,... | collective-permute-start | bytes 2752520 | tf_op jit(solution)/shard_map/ppermute | solution.py:23
  24.4 47.7 %collective-permute-start.4 = (bf16[1024,448]{0,1:T(8,128)(2,1)}, bf16[1024,448]{0,1:T(8,128)(2,1)}, u32[]{:S(2)}, u32[]{:S(2)}) collective-permute-start(bf16[1024,448]{0,1:T(8,128)(2,1)} %bitcast), channel_id=1, source_target_pairs={} | collective-permute-start | bytes 2752520 | tf_op jit(solution)/shard_map/ppermute | solution.py:23
  42.4 1.1 copy-start.2
  55.0 5.5 %copy-start = (bf16[1,448,448]{2,1,0:T(8,128)(2,1)}, bf16[1,448,448]{2,1,0:T(8,128)(2,1)S(1)}, u32[]{:S(2)}) copy-start(bf16[1,448,448]{2,1,0:T(8,128)(2,1)S(1)} %copy.16) | copy-start | bytes 1204228
  58.3 9.4 %copy-start.9 = (bf16[1,448,448]{2,1,0:T(8,128)(2,1)}, bf16[1,448,448]{2,1,0:T(8,128)(2,1)S(1)}, u32[]{:S(2)}) copy-start(bf16[1,448,448]{2,1,0:T(8,128)(2,1)S(1)} %copy.18) | copy-start | bytes 1204228
  69.7 2.4 %copy-start.15 = (bf16[1024,448]{0,1:T(8,128)(2,1)}, bf16[1024,448]{0,1:T(8,128)(2,1)S(1)}, u32[]{:S(2)}) copy-start(bf16[1024,448]{0,1:T(8,128)(2,1)S(1)} %fusion.27) | copy-start | bytes 2752516
  76.1 2.8 %copy-start.3 = (bf16[3,448,448]{2,1,0:T(8,128)(2,1)S(1)}, bf16[3,448,448]{2,1,0:T(8,128)(2,1)}, u32[]{:S(2)}) copy-start(bf16[3,448,448]{2,1,0:T(8,128)(2,1)} %copy-done.2) | copy-start | bytes 3612676
  78.6 2.2 %copy-start.7 = (f32[448,1024]{1,0:T(8,128)S(1)}, f32[448,1024]{1,0:T(8,128)}, u32[]{:S(2)}) copy-start(f32[448,1024]{1,0:T(8,128)} %fusion.54) | copy-start | bytes 5505028
  78.6 79.7 %reduce-scatter.7.cloned.1.call-start = ((), (), s32[]{:S(2)}) async-start(), calls=%async_computation.3 | async-start | bytes 1576960
  78.9 2.0 copy-start.16
  80.9 6.1 %copy-start.5 = (bf16[1,1024,448]{1,2,0:T(8,128)(2,1)S(1)}, bf16[1,1024,448]{1,2,0:T(8,128)(2,1)}, u32[]{:S(2)}) copy-start(bf16[1,1024,448]{1,2,0:T(8,128)(2,1)} %param.4) | copy-start | bytes 2752516
  84.2 3.6 %copy-start.11 = (bf16[1024,448]{0,1:T(8,128)(2,1)}, bf16[1024,448]{0,1:T(8,128)(2,1)S(1)}, u32[]{:S(2)}) copy-start(bf16[1024,448]{0,1:T(8,128)(2,1)S(1)} %fusion.17) | copy-start | bytes 2752516
  84.2 20.3 %collective-permute-start.6 = (bf16[1024,448]{0,1:T(8,128)(2,1)S(1)}, bf16[1024,448]{0,1:T(8,128)(2,1)S(1)}, u32[]{:S(2)}, u32[]{:S(2)}) collective-permute-start(bf16[1024,448]{0,1:T(8,128)(2,1)S(1)} %fusion.17), channel_id=1, source_target_pairs={{0,8},{4,12},{1,9},{5,13},{2,10},{6,14},{3,11},{7,15},{16,24},{20,... | collective-permute-start | bytes 2752520 | tf_op jit(solution)/shard_map/ppermute | solution.py:23
  85.7 43.5 %collective-permute-start.5 = (bf16[1024,448]{0,1:T(8,128)(2,1)S(1)}, bf16[1024,448]{0,1:T(8,128)(2,1)S(1)}, u32[]{:S(2)}, u32[]{:S(2)}) collective-permute-start(bf16[1024,448]{0,1:T(8,128)(2,1)S(1)} %fusion.17), channel_id=1, source_target_pairs={{8,0},{12,4},{9,1},{13,5},{10,2},{14,6},{11,3},{15,7},{24,16},{28,... | collective-permute-start | bytes 2752520 | tf_op jit(solution)/shard_map/ppermute | solution.py:23
  104.5 0.9 copy-start.17
  129.2 0.9 copy-start.13
  132.1 2.5 %copy-start.8 = (bf16[1,448,448]{2,1,0:T(8,128)(2,1)S(1)}, bf16[1,448,448]{2,1,0:T(8,128)(2,1)}, u32[]{:S(2)}) copy-start(bf16[1,448,448]{2,1,0:T(8,128)(2,1)} %copy.17) | copy-start | bytes 1204228
  132.1 2.5 %copy-start.12 = (bf16[1024,448]{0,1:T(8,128)(2,1)S(1)}, bf16[1024,448]{0,1:T(8,128)(2,1)}, u32[]{:S(2)}) copy-start(bf16[1024,448]{0,1:T(8,128)(2,1)} %copy-done.11) | copy-start | bytes 2752516
  134.7 1.0 copy-start.1
  134.7 1.3 copy-start.14
  136.0 1.2 copy-start.6
  136.0 1.3 copy-start.10
  136.0 1.7 copy-start.18
Sparse Core Ops, SparseCore 0:
  10.1 32.9 all-gather.1
  78.7 23.4 reduce-scatter.8
  134.8 23.4 reduce-scatter.6
